TPU v7x, 32 devices: a whole 2x2x4 slice. The times are simulated.
32 devices in a mesh: row: 4 (over y, core), col: 8 (over z, x).
Axes of the slice: x: 2, y: 2, z: 4, core: 2. Of those that a mesh axis runs over, the one named last changes fastest.
Arguments:
- states_now: float32 [40, 4096], P(None, ('col', 'row')), may hold values from -60 to 60
- states_next: float32 [40, 4096], P(None, ('row', 'col')), may hold values from -60 to 60
- states_last: float32 [40, 4096], P(None, ('col', 'row')), may hold values from -60 to 60
- payoff_now: bfloat16 [64, 4096], P(None, ('col', 'row')), may hold values from 0 to 2
- payoff_next: bfloat16 [64, 4096], P(None, ('row', 'col')), may hold values from 0 to 2
- payoff_last: bfloat16 [64, 4096], P(None, ('col', 'row')), may hold values from 0 to 2
Outputs:
- value_next: float32 [64, 4096], P(None, ('row', 'col'))
- value_now: float32 [64, 4096], P(None, ('col', 'row'))
All inputs are finite; a program needn't handle non-finite values.
Results may differ from a plain program's by a relative error of at most 0.0003.
Values sent between devices are 32-bit elements; how exact they have to be, the bound alone decides.
No kernel may reach another device: no remote copies, remote signals or barrier semaphores. Data moves between devices by JAX's collectives and lax.ppermute only.
A program may use at most 128 MiB of HBM per device.

v0:
```python
import math
import jax
import jax.numpy as jnp
from jax import lax
from jax.sharding import PartitionSpec as P


def merged(array, axis, combine):
    everything = jax.tree.map(lambda part: lax.all_gather(part, axis), array)
    first = jax.tree.map(lambda part: part[0], everything)

    def lap(k, so_far):
        return combine(so_far, jax.tree.map(lambda part: part[k], everything))

    return lax.fori_loop(1, lax.axis_size(axis), lap, first)


def log_kernel(row_states, col_states, row_norms, col_norms):
    cross_term = lax.dot_general(
        row_states,
        col_states,
        (((0,), (0,)), ((), ())),
        precision=lax.Precision.HIGHEST,
        preferred_element_type=jnp.float32,
    )
    return cross_term - 0.5 * row_norms[:, None] - 0.5 * col_norms[None, :]


def log_blocks(row_states, col_states):
    factors, points = row_states.shape
    block_rows = math.gcd(points, 512)
    block_count = points // block_rows
    blocks = row_states.reshape(factors, block_count, block_rows).transpose(1, 0, 2)
    norms = jnp.sum(row_states * row_states, axis=0).reshape(block_count, block_rows)
    col_norms = jnp.sum(col_states * col_states, axis=0)

    def build(block_item):
        row_piece, piece_norms = block_item
        return log_kernel(row_piece, col_states, piece_norms, col_norms)

    return lax.map(build, (blocks, norms))


def local_stats(log_weight):
    col_peak = jnp.max(log_weight, axis=(0, 1))
    col_sum = jnp.sum(jnp.exp(log_weight - col_peak[None, None, :]), axis=(0, 1))
    return (col_peak, col_sum)


def join_stats(earlier_pair, later_pair):
    new_peak = jnp.maximum(earlier_pair[0], later_pair[0])
    joined = earlier_pair[1] * jnp.exp(earlier_pair[0] - new_peak) + later_pair[1] * jnp.exp(
        later_pair[0] - new_peak
    )
    return (new_peak, joined)


def stats_row(col_peak, col_sum):
    global_peak = lax.pmax(col_peak, "row")
    global_sum = lax.psum(col_sum * jnp.exp(col_peak - global_peak), "row")
    return (global_peak, global_sum)


def stats_col(col_peak, col_sum):
    return merged((col_peak, col_sum), "col", join_stats)


def continuation(log_weight, later_value, col_peak, col_sum):
    scaled = (later_value / col_sum[None, :]).astype(jnp.bfloat16)

    def project(weight_block):
        kernel = jnp.exp(weight_block - col_peak[None, :]).astype(jnp.bfloat16)
        return lax.dot_general(
            scaled, kernel, (((1,), (1,)), ((), ())), preferred_element_type=jnp.float32
        )

    pieces = lax.map(project, log_weight)
    block_count, block_rows = (log_weight.shape[0], log_weight.shape[1])
    return pieces.transpose(1, 0, 2).reshape(scaled.shape[0], block_count * block_rows)


def per_device(states_now, states_next, states_last, payoff_now, payoff_next, payoff_last):
    own_points = payoff_next.shape[1]
    later_states, later_values = (
        lax.all_gather(states_last, "row", axis=1, tiled=True),
        lax.all_gather(payoff_last.astype(jnp.float32), "row", axis=1, tiled=True),
    )
    next_rows, next_payoff = (
        lax.all_gather(states_next, "col", axis=1, tiled=True),
        lax.all_gather(payoff_next.astype(jnp.float32), "col", axis=1, tiled=True),
    )
    weights = log_blocks(next_rows, later_states)
    col_peak, col_sum = local_stats(weights)
    col_peak, col_sum = stats_row(col_peak, col_sum)
    partial_value = continuation(weights, later_values, col_peak, col_sum)
    whole_sum = lax.psum(partial_value, "col")
    value_block = jnp.maximum(next_payoff, whole_sum)
    value_next = lax.dynamic_slice_in_dim(
        value_block, lax.axis_index("col") * own_points, own_points, 1
    )
    now_rows = lax.all_gather(states_now, "row", axis=1, tiled=True)
    weights = log_blocks(now_rows, next_rows)
    col_peak, col_sum = local_stats(weights)
    col_peak, col_sum = stats_col(col_peak, col_sum)
    partial_value = continuation(weights, value_block, col_peak, col_sum)
    own_block = lax.psum_scatter(partial_value, "row", scatter_dimension=1, tiled=True)
    value_now = jnp.maximum(payoff_now.astype(jnp.float32), own_block)
    return (value_next, value_now)


def solution(mesh):
    in_specs = (
        P(None, ("col", "row")),
        P(None, ("row", "col")),
        P(None, ("col", "row")),
        P(None, ("col", "row")),
        P(None, ("row", "col")),
        P(None, ("col", "row")),
    )
    out_specs = (P(None, ("row", "col")), P(None, ("col", "row")))
    return jax.shard_map(
        per_device, mesh=mesh, in_specs=in_specs, out_specs=out_specs, check_vma=False
    )
```

profile of v0, /device:TPU:0, one launch (start us, length us, event | category | flops | bytes accessed | tf_op | source)
XLA Modules:
  0.0 198.5 jit_solution(9412907396690079252)
XLA Ops:
  7.2 0.0 all-reduce.2.cloned.1.call-start
  7.2 32.6 %all_gather.28 = f32[40,1024]{1,0:T(8,128)S(1)} all-gather(f32[40,128]{1,0:T(8,128)} %param.13), channel_id=1, replica_groups=mesh['row'=4,'col'=8] {'col'}, dimensions={1}, use_global_device_ids=true | all-gather | bytes 184320 | tf_op jit(solution)/shard_map/all_gather | solution.py:89
  39.8 0.1 reshape.54
  40.0 5.5 %all_gather.29 = f32[40,512]{1,0:T(8,128)S(1)} all-gather(f32[40,128]{1,0:T(8,128)} %param.14), channel_id=1, replica_groups=mesh['row'=4,'col'=8] {'row'}, dimensions={1}, use_global_device_ids=true | all-gather | bytes 102400 | tf_op jit(solution)/shard_map/all_gather | solution.py:85
  45.5 2.4 %while.45 = (s32[]{:T(128)}, f32[2,512,512]{2,1,0:T(8,128)S(1)}, f32[2,40,512]{2,0,1:T(2,128)S(1)}, f32[40,512]{1,0:T(8,128)S(1)}, f32[2,512]{1,0:T(2,128)S(1)}, /*index=5*/f32[512]{0:T(512)S(1)}, s32[]{:T(128)}) while((s32[]{:T(128)}, f32[2,512,512]{2,1,0:T(8,128)S(1)}, f32[2,40,512]{2,0,1:T(2,128)S(1)}, f32[40,512]{1,0:T(8,128)S(1)}, ...), condition=%wide.region_3.4_spmd, body=%wide.region_2.3_spmd.sunk | while | flops 126354432 | bytes 1388633 | solution.py:41
  45.5 0.1 constant_dynamic-slice_fusion.6
  45.6 1.1 fusion.23
  46.7 0.1 constant_dynamic-slice_fusion.6
  46.8 1.1 fusion.23
  47.9 0.0 copy-start.1
  47.9 0.2 reduce_max.18
  48.1 0.4 exponential_reduce_fusion.1
  48.5 7.1 %pmax.7 = f32[512]{0:T(512)S(1)} all-reduce(f32[512]{0:T(512)S(1)} %reduce_max.18), channel_id=1, replica_groups=mesh['row'=4,'col'=8] {'row'}, use_global_device_ids=true, to_apply=%region_5.6 | all-reduce | flops 512 | bytes 4096 | tf_op jit(solution)/shard_map/pmax | solution.py:59
  55.6 5.9 %psum.14 = f32[512]{0:T(512)S(1)} all-reduce(f32[512]{0:T(512)S(1)} %exponential_multiply_fusion), channel_id=1, replica_groups=mesh['row'=4,'col'=8] {'row'}, use_global_device_ids=true, to_apply=%region_7.8 | all-reduce | flops 512 | bytes 4096 | tf_op jit(solution)/shard_map/psum | solution.py:60
  61.5 0.0 copy-done.1
  61.5 5.4 %all_gather.30 = f32[64,512]{1,0:T(8,128)S(1)} all-gather(f32[64,128]{1,0:T(8,128)S(1)} %convert_element_type.23), channel_id=1, replica_groups=mesh['row'=4,'col'=8] {'row'}, dimensions={1}, use_global_device_ids=true | all-gather | bytes 163840 | tf_op jit(solution)/shard_map/all_gather | solution.py:86
  66.9 0.0 copy-start
  66.9 0.6 while.46
  66.9 0.3 fusion.26
  67.3 0.3 fusion.26
  67.6 0.7 copy.14
  68.3 0.0 all-reduce.2.cloned.1.call-update
  68.3 0.0 reduce-scatter.2.cloned.1.call-start
  68.4 0.0 copy-done
  68.4 5.3 %all_gather.31 = f32[40,512]{1,0:T(8,128)S(1)} all-gather(f32[40,128]{1,0:T(8,128)S(1)} %copy-done), channel_id=1, replica_groups=mesh['row'=4,'col'=8] {'row'}, dimensions={1}, use_global_device_ids=true | all-gather | bytes 102400 | tf_op jit(solution)/shard_map/all_gather | solution.py:101
  73.7 0.0 copy-start.2
  73.7 2.0 fusion.12
  75.7 0.3 exponential_reduce_fusion
  76.0 30.6 %all-gather.1 = f32[8192]{0:T(1024)S(1)} all-gather(f32[1024]{0:T(1024)S(1)} %exponential_reduce_fusion), channel_id=3, replica_groups=mesh['row'=4,'col'=8] {'col'}, dimensions={0}, use_global_device_ids=true | all-gather | bytes 36864 | tf_op jit(solution)/shard_map/all_gather | solution.py:9
  106.6 30.7 %all-gather = f32[8192]{0:T(1024)S(1)} all-gather(f32[1024]{0:T(1024)S(1)} %get-tuple-element.279), channel_id=2, replica_groups=mesh['row'=4,'col'=8] {'col'}, dimensions={0}, use_global_device_ids=true | all-gather | bytes 36864 | tf_op jit(solution)/shard_map/all_gather | solution.py:9
  137.4 0.0 copy-start.3
  137.4 0.4 while.47
  137.8 0.0 copy-done.2
  137.8 30.7 %all_gather.27 = f32[64,1024]{1,0:T(8,128)S(1)} all-gather(f32[64,128]{1,0:T(8,128)S(1)} %convert_element_type.22), channel_id=1, replica_groups=mesh['row'=4,'col'=8] {'col'}, dimensions={1}, use_global_device_ids=true | all-gather | bytes 294912 | tf_op jit(solution)/shard_map/all_gather | solution.py:90
  168.6 0.0 all-reduce.2.cloned.1.call-done
  168.6 1.0 max.18
  169.6 1.1 fusion.9
  170.6 0.0 reduce-scatter.2.cloned.1.call-update
  170.7 0.6 constant_dynamic-slice_fusion.3
  171.3 19.0 %reduce-scatter.2.cloned.1.call-done = f32[64,128]{1,0:T(8,128)} async-done(((f32[64,512]{1,0:T(8,128)}), f32[64,128]{1,0:T(8,128)}) %reduce-scatter.2.cloned.1.call-update) | async-done | bytes 32784 | tf_op jit(solution)/shard_map/reduce_scatter | solution.py:106
  190.3 0.0 copy-done.3
  190.3 1.4 convert_maximum_fusion
  (34 shorter events, 0.4 us)
Async XLA Ops:
  7.2 161.4 %all-reduce.2.cloned.1.call-start = ((), (), s32[]{:S(2)}) async-start(), calls=%async_computation.1 | async-start | bytes 524288 | tf_op jit(solution)/shard_map/psum | solution.py:96
  47.9 13.6 %copy-start.1 = (bf16[64,128]{1,0:T(8,128)(2,1)S(1)}, bf16[64,128]{1,0:T(8,128)(2,1)}, u32[]{:S(2)}) copy-start(bf16[64,128]{1,0:T(8,128)(2,1)} %param.17) | copy-start | bytes 49156
  66.9 1.5 copy-start
  68.3 122.0 %reduce-scatter.2.cloned.1.call-start = ((), (), s32[]{:S(2)}) async-start(), calls=%async_computation.2 | async-start | bytes 163840 | tf_op jit(solution)/shard_map/reduce_scatter | solution.py:106
  73.7 64.1 %copy-start.2 = (bf16[64,128]{1,0:T(8,128)(2,1)S(1)}, bf16[64,128]{1,0:T(8,128)(2,1)}, u32[]{:S(2)}) copy-start(bf16[64,128]{1,0:T(8,128)(2,1)} %param.16) | copy-start | bytes 49156
  137.4 52.9 %copy-start.3 = (bf16[64,128]{1,0:T(8,128)(2,1)S(1)}, bf16[64,128]{1,0:T(8,128)(2,1)}, u32[]{:S(2)}) copy-start(bf16[64,128]{1,0:T(8,128)(2,1)} %param.15) | copy-start | bytes 49156
Sparse Core Ops, SparseCore 0:
  68.4 71.0 all-reduce.1
  170.8 19.4 reduce-scatter.1
where the time goes:
time: 199 us
  blocking collectives  154 us (77%)
  waiting for transfers between devices  19 us (10%)
  between operations  14.2 us (7%)
  matrix products  5.77 us (3%)
  other arithmetic  3.48 us (2%)
    all_gather x2, blocking collectives, merged(): everything = jax.tree.map(lambda part: lax.all_gather(part, axis), array)  61.3 us
    all_gather x1, blocking collectives, per_device(): lax.all_gather(states_next, 'col', axis=1, tiled=True)  32.6 us
    all_gather x1, blocking collectives, per_device(): lax.all_gather(payoff_next.astype(jnp.float32), 'col', axis=1, tiled=True)  30.7 us
    reduce_scatter x1, waiting for transfers between devices, per_device(): lax.psum_scatter(partial_value, 'row', scatter_dimension=1, tiled=True)  19 us
    pmax x1, blocking collectives, stats_row(): global_peak = lax.pmax(col_peak, 'row')  7.11 us
    psum x1, blocking collectives, stats_row(): global_sum = lax.psum(col_sum * jnp.exp(col_peak - global_peak), 'row')  5.88 us
    all_gather x1, blocking collectives, per_device(): lax.all_gather(states_last, 'row', axis=1, tiled=True)  5.49 us
    all_gather x1, blocking collectives, per_device(): lax.all_gather(payoff_last.astype(jnp.float32), 'row', axis=1, tiled=True)  5.42 us
  transfers between devices with their start and end apart: 2, of which 1 were waited for; matrix products, arithmetic and copies ran while one was open for 2% of the time, Pallas kernels for 0%

commit v1 on v0

--- a/solution.py
+++ b/solution.py
@@ -3,6 +3,12 @@
 import jax.numpy as jnp
 from jax import lax
 from jax.sharding import PartitionSpec as P
+
+
+def match_run(slab_in):
+    return jnp.concatenate(
+        lax.all_to_all(jnp.stack([slab_in] * lax.axis_size("col")), "col", 0, 0), axis=1
+    )
 
 
 def merged(array, axis, combine):
@@ -87,7 +93,7 @@
     )
     next_rows, next_payoff = (
         lax.all_gather(states_next, "col", axis=1, tiled=True),
-        lax.all_gather(payoff_next.astype(jnp.float32), "col", axis=1, tiled=True),
+        match_run(payoff_next.astype(jnp.float32)),
     )
     weights = log_blocks(next_rows, later_states)
     col_peak, col_sum = local_stats(weights)

time: 199 us -> 175 us (0.88)
  blocking collectives: 154 us -> 124 us
  starting transfers between devices: 0.08 us -> 5.55 us
    all_gather x1 -> x0, blocking collectives: 30.7 us -> none  [per_device(): lax.all_gather(payoff_next.astype(jnp.float32), 'col', axis=1, tiled=True)]
    all_to_all x0 -> x1, starting transfers between devices: none -> 5.48 us  [match_run(): lax.all_to_all(jnp.stack([slab_in] * lax.axis_size('col')), 'col', 0, 0)]
  transfers between devices with their start and end apart: 2 -> 3, of which waited for: 1 -> 1; matrix products, arithmetic and copies ran while one was open for 2% -> 2% of each run, Pallas kernels for 0% -> 0%
where the time goes in v1:
time: 175 us
  blocking collectives  124 us (71%)
  waiting for transfers between devices  19.2 us (11%)
  between operations  14.2 us (8%)
  matrix products  5.76 us (3%)
  starting transfers between devices  5.55 us (3%)
  other arithmetic  3.49 us (2%)
  local copies, waits for them, and re-layouts  2.5 us (1%)
    all_gather x2, blocking collectives, merged(): everything = jax.tree.map(lambda part: lax.all_gather(part, axis), array)  61.8 us
    all_gather x1, blocking collectives, per_device(): lax.all_gather(states_next, 'col', axis=1, tiled=True)  32.6 us
    reduce_scatter x1, waiting for transfers between devices, per_device(): lax.psum_scatter(partial_value, 'row', scatter_dimension=1, tiled=True)  19.1 us
    pmax x1, blocking collectives, stats_row(): global_peak = lax.pmax(col_peak, 'row')  7.11 us
    psum x1, blocking collectives, stats_row(): global_sum = lax.psum(col_sum * jnp.exp(col_peak - global_peak), 'row')  5.88 us
    all_gather x1, blocking collectives, per_device(): lax.all_gather(states_last, 'row', axis=1, tiled=True)  5.49 us
    all_to_all x1, starting transfers between devices, match_run(): lax.all_to_all(jnp.stack([slab_in] * lax.axis_size('col')), 'col', 0, 0)  5.48 us
    all_gather x1, blocking collectives, per_device(): lax.all_gather(payoff_last.astype(jnp.float32), 'row', axis=1, tiled=True)  5.42 us
  transfers between devices with their start and end apart: 3, of which 1 were waited for; matrix products, arithmetic and copies ran while one was open for 2% of the time, Pallas kernels for 0%

profile of v1, /device:TPU:0, one launch (start us, length us, event | category | flops | bytes accessed | tf_op | source)
XLA Modules:
  0.0 174.5 jit_solution(16604641671554591684)
XLA Ops:
  7.2 0.0 all-reduce.2.cloned.1.call-start
  7.2 32.6 %all_gather.24 = f32[40,1024]{1,0:T(8,128)S(1)} all-gather(f32[40,128]{1,0:T(8,128)} %param.13), channel_id=1, replica_groups=mesh['row'=4,'col'=8] {'col'}, dimensions={1}, use_global_device_ids=true | all-gather | bytes 184320 | tf_op jit(solution)/shard_map/all_gather | solution.py:95
  39.8 0.1 reshape.64
  40.0 5.5 %all_gather.25 = f32[40,512]{1,0:T(8,128)S(1)} all-gather(f32[40,128]{1,0:T(8,128)} %param.14), channel_id=1, replica_groups=mesh['row'=4,'col'=8] {'row'}, dimensions={1}, use_global_device_ids=true | all-gather | bytes 102400 | tf_op jit(solution)/shard_map/all_gather | solution.py:91
  45.5 2.4 %while.45 = (s32[]{:T(128)}, f32[2,512,512]{2,1,0:T(8,128)S(1)}, f32[2,40,512]{2,0,1:T(2,128)S(1)}, f32[40,512]{1,0:T(8,128)S(1)}, f32[2,512]{1,0:T(2,128)S(1)}, /*index=5*/f32[512]{0:T(512)S(1)}, s32[]{:T(128)}) while((s32[]{:T(128)}, f32[2,512,512]{2,1,0:T(8,128)S(1)}, f32[2,40,512]{2,0,1:T(2,128)S(1)}, f32[40,512]{1,0:T(8,128)S(1)}, ...), condition=%wide.region_3.4_spmd, body=%wide.region_2.3_spmd.sunk | while | flops 126354432 | bytes 1388633 | solution.py:47
  45.5 0.1 constant_dynamic-slice_fusion.6
  45.6 1.1 fusion.24
  46.7 0.1 constant_dynamic-slice_fusion.6
  46.8 1.1 fusion.24
  47.9 0.0 copy-start.1
  47.9 0.2 reduce_max.18
  48.1 0.4 exponential_reduce_fusion.1
  48.5 7.1 %pmax.7 = f32[512]{0:T(512)S(1)} all-reduce(f32[512]{0:T(512)S(1)} %reduce_max.18), channel_id=1, replica_groups=mesh['row'=4,'col'=8] {'row'}, use_global_device_ids=true, to_apply=%region_5.6 | all-reduce | flops 512 | bytes 4096 | tf_op jit(solution)/shard_map/pmax | solution.py:65
  55.6 5.9 %psum.14 = f32[512]{0:T(512)S(1)} all-reduce(f32[512]{0:T(512)S(1)} %exponential_multiply_fusion), channel_id=1, replica_groups=mesh['row'=4,'col'=8] {'row'}, use_global_device_ids=true, to_apply=%region_7.8 | all-reduce | flops 512 | bytes 4096 | tf_op jit(solution)/shard_map/psum | solution.py:66
  61.5 0.0 copy-done.1
  61.5 5.4 %all_gather.26 = f32[64,512]{1,0:T(8,128)S(1)} all-gather(f32[64,128]{1,0:T(8,128)S(1)} %convert_element_type.23), channel_id=1, replica_groups=mesh['row'=4,'col'=8] {'row'}, dimensions={1}, use_global_device_ids=true | all-gather | bytes 163840 | tf_op jit(solution)/shard_map/all_gather | solution.py:92
  66.9 0.0 copy-start.2
  66.9 0.0 copy-start
  66.9 0.6 while.46
  66.9 0.3 fusion.27
  67.3 0.3 fusion.27
  67.6 0.7 copy.18
  68.3 0.0 all-reduce.2.cloned.1.call-update
  68.3 0.0 copy-done.2
  68.3 0.7 stack.2
  69.0 5.5 %all-to-all-start = ((f32[8,64,128]{2,1,0:T(8,128)}), f32[8,64,128]{2,1,0:T(8,128)S(1)}, u32[]{:S(2)}, u32[]{:S(2)}) async-start(f32[8,64,128]{2,1,0:T(8,128)} %stack.2), calls=%async_computation | async-start | bytes 524288 | tf_op jit(solution)/shard_map/all_to_all | solution.py:10
  74.5 0.0 reduce-scatter.2.cloned.1.call-start
  74.6 0.0 copy-done
  74.6 5.3 %all_gather.27 = f32[40,512]{1,0:T(8,128)S(1)} all-gather(f32[40,128]{1,0:T(8,128)S(1)} %copy-done), channel_id=1, replica_groups=mesh['row'=4,'col'=8] {'row'}, dimensions={1}, use_global_device_ids=true | all-gather | bytes 102400 | tf_op jit(solution)/shard_map/all_gather | solution.py:107
  79.9 2.0 %fusion.12 = (f32[1024]{0:T(1024)S(1)}, f32[512,1024]{1,0:T(8,128)S(1)}) fusion(f32[1024]{0:T(1024)S(1)} %broadcast_multiply_fusion.1, f32[512]{0:T(512)S(1)} %broadcast_multiply_fusion.2, f32[40,512]{1,0:T(8,128)S(1)} %all_gather.27, f32[40,1024]{1,0:T(8,128)S(1)} %all_gather.24), kind=kOutput, calls=%fused_computation.36 | convolution fusion | flops 253230080 | bytes 2353152 | tf_op jit(solution)/shard_map/while/body/eval_jaxpr/dot_general | solution.py:25
  81.9 0.3 exponential_reduce_fusion
  82.2 0.0 copy-start.3
  82.2 31.1 %all-gather.1 = f32[8192]{0:T(1024)S(1)} all-gather(f32[1024]{0:T(1024)S(1)} %exponential_reduce_fusion), channel_id=3, replica_groups=mesh['row'=4,'col'=8] {'col'}, dimensions={0}, use_global_device_ids=true | all-gather | bytes 36864 | tf_op jit(solution)/shard_map/all_gather | solution.py:15
  113.4 30.6 %all-gather = f32[8192]{0:T(1024)S(1)} all-gather(f32[1024]{0:T(1024)S(1)} %get-tuple-element.285), channel_id=2, replica_groups=mesh['row'=4,'col'=8] {'col'}, dimensions={0}, use_global_device_ids=true | all-gather | bytes 36864 | tf_op jit(solution)/shard_map/all_gather | solution.py:15
  144.0 0.4 while.47
  144.4 0.0 all-reduce.2.cloned.1.call-done
  144.5 0.0 all-to-all-done
  144.5 1.0 bitcast_maximum_fusion
  145.5 1.1 fusion.9
  146.6 0.0 reduce-scatter.2.cloned.1.call-update
  146.6 0.6 constant_dynamic-slice_fusion.3
  147.2 19.1 %reduce-scatter.2.cloned.1.call-done = f32[64,128]{1,0:T(8,128)} async-done(((f32[64,512]{1,0:T(8,128)}), f32[64,128]{1,0:T(8,128)}) %reduce-scatter.2.cloned.1.call-update) | async-done | bytes 32784 | tf_op jit(solution)/shard_map/reduce_scatter | solution.py:112
  166.3 0.0 copy-done.3
  166.3 1.4 convert_maximum_fusion
  (33 shorter events, 0.4 us)
Async XLA Ops:
  7.2 137.3 %all-reduce.2.cloned.1.call-start = ((), (), s32[]{:S(2)}) async-start(), calls=%async_computation.2 | async-start | bytes 524288 | tf_op jit(solution)/shard_map/psum | solution.py:102
  47.9 13.6 %copy-start.1 = (bf16[64,128]{1,0:T(8,128)(2,1)S(1)}, bf16[64,128]{1,0:T(8,128)(2,1)}, u32[]{:S(2)}) copy-start(bf16[64,128]{1,0:T(8,128)(2,1)} %param.17) | copy-start | bytes 49156
  66.9 1.4 copy-start.2
  66.9 7.7 %copy-start = (f32[40,128]{1,0:T(8,128)S(1)}, f32[40,128]{1,0:T(8,128)}, u32[]{:S(2)}) copy-start(f32[40,128]{1,0:T(8,128)} %param.12) | copy-start | bytes 61444
  69.0 75.4 %all-to-all-start = ((f32[8,64,128]{2,1,0:T(8,128)}), f32[8,64,128]{2,1,0:T(8,128)S(1)}, u32[]{:S(2)}, u32[]{:S(2)}) async-start(f32[8,64,128]{2,1,0:T(8,128)} %stack.2), calls=%async_computation | async-start | bytes 524288 | tf_op jit(solution)/shard_map/all_to_all | solution.py:10
  74.5 91.8 %reduce-scatter.2.cloned.1.call-start = ((), (), s32[]{:S(2)}) async-start(), calls=%async_computation.3 | async-start | bytes 163840 | tf_op jit(solution)/shard_map/reduce_scatter | solution.py:112
  82.2 84.1 %copy-start.3 = (bf16[64,128]{1,0:T(8,128)(2,1)S(1)}, bf16[64,128]{1,0:T(8,128)(2,1)}, u32[]{:S(2)}) copy-start(bf16[64,128]{1,0:T(8,128)(2,1)} %param.15) | copy-start | bytes 49156
Sparse Core Ops, SparseCore 0:
  68.4 72.5 all-reduce.1
  146.7 19.5 reduce-scatter.1
